TPU v7x, 256 devices: a whole 4x4x8 slice. The times are simulated.
256 devices in a mesh: dp: 16 (over y, z_hi), expert: 8 (over x, core), tensor: 2 (over z_lo).
Axes of the slice: x: 4, y: 4, z: 8 (z_hi: 4, z_lo: 2; z = z_hi * 2 + z_lo), core: 2. Of those that a mesh axis runs over, the one named last changes fastest.
Arguments:
- tokens: bfloat16 [2048, 5120], P('dp', 'tensor'), may hold values from -6 to 6
- routes: int32 [2048, 6], P('dp'), may hold values from 0 to 15, all different within a row; in each aligned block of 128 rows (0 to 127, 128 to 255, ...) at most 72 rows name the same one
- route_weights: float32 [2048, 6], P('dp'), may hold values from 0.05 to 0.5
- gate_weight: bfloat16 [16, 1536, 5120], P('dp', 'expert', 'tensor'), may hold values from -0.078125 to 0.078125
- up_weight: bfloat16 [16, 1536, 5120], P('dp', 'expert', 'tensor'), may hold values from -0.078125 to 0.078125
- down_weight: bfloat16 [16, 1536, 5120], P('dp', 'expert', 'tensor'), may hold values from -0.15625 to 0.15625
- cotangent: bfloat16 [2048, 5120], P('dp', 'tensor'), may hold values from -6 to 6
Outputs:
- layer_out: bfloat16 [2048, 5120], P('dp', 'tensor')
- token_grad: bfloat16 [2048, 5120], P('dp', 'tensor')
- gate_grad: float32 [16, 1536, 5120], P('dp', 'expert', 'tensor')
- up_grad: float32 [16, 1536, 5120], P('dp', 'expert', 'tensor')
- down_grad: float32 [16, 1536, 5120], P('dp', 'expert', 'tensor')
Inputs may be any that keep to these rules, and one draw needn't show every extreme that they name: `routes`: each row names 6 different experts. In the rows of one index of dp (aligned blocks of 128 rows) no expert is named by more than 72 rows, a bound that some block reaches.
All inputs are finite; a program needn't handle non-finite values.
Results may differ from a plain program's by a relative error of at most 0.023.
Values may be sent and summed in bfloat16 or wider, within the bound.
A program may use at most 128 MiB of HBM per device.

v0:
```python
import jax
import jax.numpy as jnp
from jax import lax
from jax.sharding import PartitionSpec as P


def body(tokens, routes, route_weights, gate_weight, up_weight, down_weight, cotangent):
    dp_count = lax.axis_size("dp")
    hidden_split = lax.axis_size("expert")
    gate_weight, up_weight, down_weight = (gate_weight[0], up_weight[0], down_weight[0])
    hidden_share, half_width = gate_weight.shape
    tok_rows, top_count = routes.shape
    experts = dp_count
    capacity = min(tok_rows, 3 * tok_rows * top_count // (2 * experts))
    share_rows = capacity // hidden_split
    own_rows = experts * share_rows
    pair_count = tok_rows * top_count
    flat_route = routes.T.reshape(pair_count)
    onehot = flat_route[:, None] == jnp.arange(experts, dtype=jnp.int32)[None, :]
    running = jnp.cumsum(onehot.astype(jnp.int32), axis=0) - 1
    position = jnp.sum(jnp.where(onehot, running, 0), axis=1)
    target = flat_route * capacity + position
    member = lax.axis_index("expert")
    own_index = jnp.arange(own_rows, dtype=jnp.int32)
    own_slot = own_index // share_rows * capacity + member * share_rows + own_index % share_rows
    selector = (own_slot[:, None] == target[None, :]).reshape(own_rows, top_count, tok_rows)
    weight_grid = jnp.sum(jnp.where(selector, route_weights.T[None], jnp.float32(0.0)), axis=1)
    own_weight = jnp.sum(weight_grid, axis=1, keepdims=True)
    own_place = jnp.any(selector, axis=1).astype(jnp.bfloat16)

    def select(values):
        return jnp.dot(own_place, values, preferred_element_type=jnp.float32)

    def dispatch(rows):
        arrived = lax.all_to_all(
            rows.reshape(dp_count, share_rows, half_width),
            "dp",
            split_axis=0,
            concat_axis=0,
            tiled=True,
        )
        return lax.all_gather(arrived.reshape(own_rows, half_width), "expert", axis=0, tiled=True)

    def width_sum(partial_values):
        mine = partial_values.astype(jnp.bfloat16)
        other = lax.ppermute(mine, "tensor", [(0, 1), (1, 0)])
        return mine.astype(jnp.float32) + other.astype(jnp.float32)

    def home(partial_rows):
        summed = lax.psum_scatter(
            partial_rows.astype(jnp.bfloat16), "expert", scatter_dimension=0, tiled=True
        )
        returned = lax.all_to_all(
            summed.reshape(dp_count, share_rows, half_width),
            "dp",
            split_axis=0,
            concat_axis=0,
            tiled=True,
        )
        return returned.reshape(own_rows, half_width)

    def token_sum(partial_tokens):
        part = lax.psum_scatter(
            partial_tokens.astype(jnp.bfloat16), "expert", scatter_dimension=0, tiled=True
        )
        return lax.all_gather(part, "expert", axis=0, tiled=True)

    rows = dispatch(select(tokens).astype(jnp.bfloat16))
    grad_rows = dispatch((select(cotangent) * own_weight).astype(jnp.bfloat16))
    nt = (((1,), (1,)), ((), ()))
    nn = (((1,), (0,)), ((), ()))
    tn = (((0,), (0,)), ((), ()))

    def mm(a, b, dims):
        return lax.dot_general(a, b, dims, preferred_element_type=jnp.float32)

    gate_val = width_sum(mm(rows, gate_weight, nt))
    up_val = width_sum(mm(rows, up_weight, nt))
    sigmoid_gate = jax.nn.sigmoid(gate_val)
    activated = gate_val * sigmoid_gate
    hidden = (activated * up_val).astype(jnp.bfloat16)
    expert_out = home(mm(hidden, down_weight, nn))
    out_part = mm(weight_grid.astype(jnp.bfloat16), expert_out, tn)
    layer_out = token_sum(out_part)
    hidden_grad = width_sum(mm(grad_rows, down_weight, nt))
    gate_delta = (
        hidden_grad * up_val * sigmoid_gate * (1.0 + gate_val * (1.0 - sigmoid_gate))
    ).astype(jnp.bfloat16)
    up_delta = (hidden_grad * activated).astype(jnp.bfloat16)
    input_part = mm(gate_delta, gate_weight, nn) + mm(up_delta, up_weight, nn)
    row_grad = home(input_part)
    token_grad = token_sum(mm(own_place, row_grad, tn))
    gate_grad = mm(gate_delta, rows, tn)
    up_grad = mm(up_delta, rows, tn)
    down_grad = mm(hidden, grad_rows, tn)
    return (layer_out, token_grad, gate_grad[None], up_grad[None], down_grad[None])


def solution(mesh):
    in_specs = (
        P("dp", "tensor"),
        P("dp", None),
        P("dp", None),
        P("dp", "expert", "tensor"),
        P("dp", "expert", "tensor"),
        P("dp", "expert", "tensor"),
        P("dp", "tensor"),
    )
    out_specs = (
        P("dp", "tensor"),
        P("dp", "tensor"),
        P("dp", "expert", "tensor"),
        P("dp", "expert", "tensor"),
        P("dp", "expert", "tensor"),
    )
    return jax.shard_map(body, mesh=mesh, in_specs=in_specs, out_specs=out_specs, check_vma=False)
```

profile of v0, /device:TPU:1, one launch (start us, length us, event | category | flops | bytes accessed | tf_op | source)
XLA Modules:
  0.0 376.8 jit_solution(5594621330869188232)
XLA Ops:
  7.2 0.0 copy-start
  7.2 0.0 all-gather.5.cloned.1.call-start
  7.2 0.8 fusion.12
  8.0 1.7 reduce-window.6
  9.7 0.3 slice_reduce_fusion
  10.0 0.8 fusion.11
  10.8 0.7 bitcast_add_fusion
  11.5 0.1 compare_reduce_fusion
  11.6 0.9 select_reduce_fusion
  12.5 1.4 fusion.1
  13.9 0.3 reshape.100
  14.2 45.1 %all_to_all.20 = bf16[16,9,2560]{2,1,0:T(8,128)(2,1)} all-to-all(bf16[16,9,2560]{2,1,0:T(8,128)(2,1)S(1)} %reshape.100), channel_id=1, replica_groups=mesh['dp'=16,'expert'=8,'tensor'=2] {'dp'}, dimensions={0} | all-to-all | bytes 1474560 | tf_op jit(solution)/shard_map/all_to_all | solution.py:35
  59.3 2.5 reshape.101
  61.8 0.0 all-gather.5.cloned.1.call-update
  61.8 0.0 all-gather.3.cloned.1.call-start
  61.9 1.4 convolution_convert_fusion.1
  63.3 0.3 reshape.96
  63.6 33.0 %all_to_all.21 = bf16[16,9,2560]{2,1,0:T(8,128)(2,1)} all-to-all(bf16[16,9,2560]{2,1,0:T(8,128)(2,1)S(1)} %reshape.96), channel_id=1, replica_groups=mesh['dp'=16,'expert'=8,'tensor'=2] {'dp'}, dimensions={0} | all-to-all | bytes 1474560 | tf_op jit(solution)/shard_map/all_to_all | solution.py:35
  96.6 2.5 reshape.97
  99.1 0.0 all-gather.3.cloned.1.call-update
  99.1 0.0 copy-start.7
  99.1 0.0 reduce-scatter.5.cloned.1.call-start
  99.1 2.7 all-gather.5.cloned.1.call-done
  101.9 4.7 %convolution_convert_fusion.4 = bf16[1152,192]{0,1:T(8,128)(2,1)S(1)} fusion(bf16[1152,2560]{1,0:T(8,128)(2,1)} %all-gather.5.cloned.1.call-done, bf16[1,192,2560]{2,1,0:T(8,128)(2,1)S(1)} %copy-done), kind=kOutput, calls=%fused_computation.11 | convolution fusion | flops 1132683264 | bytes 7323648 | tf_op jit(solution)/shard_map/dot_general | solution.py:75
  106.6 0.0 copy-start.11
  106.6 5.1 %collective-permute-start.2 = (bf16[1152,192]{0,1:T(8,128)(2,1)S(1)}, bf16[1152,192]{0,1:T(8,128)(2,1)}, u32[]{:S(2)}, u32[]{:S(2)}) collective-permute-start(bf16[1152,192]{0,1:T(8,128)(2,1)S(1)} %convolution_convert_fusion.4), channel_id=1, source_target_pairs={{0,1},{1,0},{2,3},{3,2},{4,5},{5,4},{6,7},{7,6},{8,9},{9,8},{10,11... | collective-permute-start | bytes 1327112 | tf_op jit(solution)/shard_map/ppermute | solution.py:46
  111.7 34.5 %all-gather.3.cloned.1.call-done = bf16[1152,2560]{1,0:T(8,128)(2,1)} async-done(((bf16[144,2560]{1,0:T(8,128)(2,1)}), bf16[1152,2560]{1,0:T(8,128)(2,1)}) %all-gather.3.cloned.1.call-update) | async-done | bytes 5898256 | tf_op jit(solution)/shard_map/all_gather | solution.py:42
  146.2 4.9 %convolution_convert_fusion.6 = bf16[1152,192]{0,1:T(8,128)(2,1)S(1)} fusion(bf16[1152,2560]{1,0:T(8,128)(2,1)} %all-gather.3.cloned.1.call-done, bf16[1,192,2560]{2,1,0:T(8,128)(2,1)S(1)} %copy-done.7), kind=kOutput, calls=%fused_computation.13 | convolution fusion | flops 1132683264 | bytes 7323648 | tf_op jit(solution)/shard_map/dot_general | solution.py:75
  151.1 1.4 collective-permute-start
  152.4 2.1 convolution_convert_fusion.5
  154.5 0.3 collective-permute-start.1
  154.8 7.9 %collective-permute-done = bf16[1152,192]{0,1:T(8,128)(2,1)S(1)} collective-permute-done((bf16[1152,192]{0,1:T(8,128)(2,1)S(1)}, bf16[1152,192]{0,1:T(8,128)(2,1)S(1)}, u32[]{:S(2)}, u32[]{:S(2)}) %collective-permute-start) | collective-permute-done | bytes 442400 | tf_op jit(solution)/shard_map/ppermute | solution.py:46
  162.7 9.5 %collective-permute-done.1 = bf16[1152,192]{0,1:T(8,128)(2,1)S(1)} collective-permute-done((bf16[1152,192]{0,1:T(8,128)(2,1)S(1)}, bf16[1152,192]{0,1:T(8,128)(2,1)S(1)}, u32[]{:S(2)}, u32[]{:S(2)}) %collective-permute-start.1) | collective-permute-done | bytes 442400 | tf_op jit(solution)/shard_map/ppermute | solution.py:46
  172.1 1.8 multiply_convert_fusion
  174.0 4.3 %convolution_convert_fusion = bf16[1152,2560]{1,0:T(8,128)(2,1)} fusion(bf16[1152,192]{0,1:T(8,128)(2,1)S(1)} %get-tuple-element.9, bf16[1,192,2560]{2,1,0:T(8,128)(2,1)S(1)} %copy-done), kind=kOutput, calls=%fused_computation.2 | convolution fusion | flops 1135411200 | bytes 7323648 | tf_op jit(solution)/shard_map/dot_general | solution.py:75
  178.3 0.0 reduce-scatter.5.cloned.1.call-update
  178.3 0.2 reduce-scatter.9.cloned.1.call-start
  178.6 0.9 copy-done.8
  179.5 1.7 fusion.6
  181.2 4.3 %fusion = bf16[1152,2560]{1,0:T(8,128)(2,1)} fusion(f32[1152,2560]{1,0:T(8,128)S(1)} %fusion.6, bf16[1152,192]{0,1:T(8,128)(2,1)S(1)} %get-tuple-element.7, bf16[1,192,2560]{2,1,0:T(8,128)(2,1)S(1)} %copy-done.10), kind=kOutput, calls=%fused_computation.1 | convolution fusion | flops 1138360320 | bytes 19120128 | tf_op jit(solution)/shard_map/dot_general | solution.py:75
  185.5 0.0 reduce-scatter.9.cloned.1.call-update
  185.5 36.0 %reduce-scatter.5.cloned.1.call-done = bf16[144,2560]{1,0:T(8,128)(2,1)} async-done(((bf16[1152,2560]{1,0:T(8,128)(2,1)}), bf16[144,2560]{1,0:T(8,128)(2,1)}) %reduce-scatter.5.cloned.1.call-update) | async-done | bytes 737296 | tf_op jit(solution)/shard_map/reduce_scatter | solution.py:50
  221.5 2.5 reshape.98
  224.0 9.3 %all-to-all-start.1 = ((bf16[16,9,2560]{2,1,0:T(8,128)(2,1)}), bf16[16,9,2560]{2,1,0:T(8,128)(2,1)}, u32[]{:S(2)}, u32[]{:S(2)}) async-start(bf16[16,9,2560]{2,1,0:T(8,128)(2,1)} %reshape.98), calls=%async_computation.2 | async-start | bytes 2621440 | tf_op jit(solution)/shard_map/all_to_all | solution.py:53
  233.3 34.4 %reduce-scatter.9.cloned.1.call-done = bf16[144,2560]{1,0:T(8,128)(2,1)} async-done(((bf16[1152,2560]{1,0:T(8,128)(2,1)}), bf16[144,2560]{1,0:T(8,128)(2,1)}) %reduce-scatter.9.cloned.1.call-update) | async-done | bytes 737296 | tf_op jit(solution)/shard_map/reduce_scatter | solution.py:50
  267.7 2.5 reshape.102
  270.2 9.3 %all-to-all-start.3 = ((bf16[16,9,2560]{2,1,0:T(8,128)(2,1)}), bf16[16,9,2560]{2,1,0:T(8,128)(2,1)S(1)}, u32[]{:S(2)}, u32[]{:S(2)}) async-start(bf16[16,9,2560]{2,1,0:T(8,128)(2,1)} %reshape.102), calls=%async_computation.6 | async-start | bytes 2621440 | tf_op jit(solution)/shard_map/all_to_all | solution.py:53
  279.5 0.0 reduce-scatter.7.cloned.1.call-start
  279.6 1.6 reshape.99
  281.2 1.2 convolution_convert_fusion.3
  282.4 0.0 reduce-scatter.7.cloned.1.call-update
  282.4 0.0 reduce-scatter.11.cloned.1.call-start
  282.5 29.5 %all-to-all-done.3 = bf16[16,9,2560]{2,1,0:T(8,128)(2,1)S(1)} async-done(((bf16[16,9,2560]{2,1,0:T(8,128)(2,1)}), bf16[16,9,2560]{2,1,0:T(8,128)(2,1)S(1)}, u32[]{:S(2)}, u32[]{:S(2)}) %all-to-all-start.3) | async-done | bytes 737312 | tf_op jit(solution)/shard_map/all_to_all | solution.py:53
  312.0 0.3 reshape.103
  312.3 1.2 convolution_convert_fusion.2
  313.5 0.0 reduce-scatter.11.cloned.1.call-update
  313.6 5.6 %convolution_bitcast_fusion = f32[1,192,2560]{2,1,0:T(8,128)} fusion(bf16[1152,192]{0,1:T(8,128)(2,1)S(1)} %get-tuple-element.9, bf16[1152,2560]{1,0:T(8,128)(2,1)} %all-gather.5.cloned.1.call-done), kind=kOutput, calls=%fused_computation.3 | convolution fusion | flops 1132462080 | bytes 8306688 | tf_op jit(solution)/shard_map/dot_general | solution.py:75
  319.2 2.7 convolution_bitcast_fusion.1
  321.9 2.7 convolution_bitcast_fusion.2
  324.6 17.2 %all_gather.13 = bf16[128,2560]{1,0:T(8,128)(2,1)S(1)} all-gather(bf16[16,2560]{1,0:T(8,128)(2,1)} %reduce-scatter.7.cloned.1.call-done), channel_id=1, replica_groups=mesh['dp'=16,'expert'=8,'tensor'=2] {'expert'}, dimensions={0}, use_global_device_ids=true | all-gather | bytes 737280 | tf_op jit(solution)/shard_map/all_gather | solution.py:66
  341.8 10.3 %reduce-scatter.11.cloned.1.call-done = bf16[16,2560]{1,0:T(8,128)(2,1)} async-done(((bf16[128,2560]{1,0:T(8,128)(2,1)}), bf16[16,2560]{1,0:T(8,128)(2,1)}) %reduce-scatter.11.cloned.1.call-update) | async-done | bytes 81936 | tf_op jit(solution)/shard_map/reduce_scatter | solution.py:63
  352.1 16.1 %all_gather.15 = bf16[128,2560]{1,0:T(8,128)(2,1)S(1)} all-gather(bf16[16,2560]{1,0:T(8,128)(2,1)} %reduce-scatter.11.cloned.1.call-done), channel_id=1, replica_groups=mesh['dp'=16,'expert'=8,'tensor'=2] {'expert'}, dimensions={0}, use_global_device_ids=true | all-gather | bytes 737280 | tf_op jit(solution)/shard_map/all_gather | solution.py:66
  368.3 0.8 copy.18
  369.1 0.8 copy.19
  (30 shorter events, 0.1 us)
Async XLA Ops:
  7.2 94.7 %copy-start = (bf16[1,192,2560]{2,1,0:T(8,128)(2,1)S(1)}, bf16[1,192,2560]{2,1,0:T(8,128)(2,1)}, u32[]{:S(2)}) copy-start(bf16[1,192,2560]{2,1,0:T(8,128)(2,1)} %param.12) | copy-start | bytes 2949124
  7.2 94.7 %all-gather.5.cloned.1.call-start = ((), (), s32[]{:S(2)}) async-start(), calls=%async_computation.11 | async-start | bytes 6635520 | tf_op jit(solution)/shard_map/all_gather | solution.py:42
  61.8 84.4 %all-gather.3.cloned.1.call-start = ((), (), s32[]{:S(2)}) async-start(), calls=%async_computation.8 | async-start | bytes 6635520 | tf_op jit(solution)/shard_map/all_gather | solution.py:42
  99.1 47.1 %copy-start.7 = (bf16[1,192,2560]{2,1,0:T(8,128)(2,1)S(1)}, bf16[1,192,2560]{2,1,0:T(8,128)(2,1)}, u32[]{:S(2)}) copy-start(bf16[1,192,2560]{2,1,0:T(8,128)(2,1)} %param.10) | copy-start | bytes 2949124
  99.1 122.4 %reduce-scatter.5.cloned.1.call-start = ((), (), s32[]{:S(2)}) async-start(), calls=%async_computation.9 | async-start | bytes 6635520 | tf_op jit(solution)/shard_map/reduce_scatter | solution.py:50
  106.6 47.9 %copy-start.11 = (bf16[1152,192]{0,1:T(8,128)(2,1)}, bf16[1152,192]{0,1:T(8,128)(2,1)S(1)}, u32[]{:S(2)}) copy-start(bf16[1152,192]{0,1:T(8,128)(2,1)S(1)} %convolution_convert_fusion.4) | copy-start | bytes 1327108
  106.6 45.8 %copy-start.9 = (bf16[1,192,2560]{2,1,0:T(8,128)(2,1)S(1)}, bf16[1,192,2560]{2,1,0:T(8,128)(2,1)}, u32[]{:S(2)}) copy-start(bf16[1,192,2560]{2,1,0:T(8,128)(2,1)} %param.11) | copy-start | bytes 2949124
  106.6 48.2 %collective-permute-start.2 = (bf16[1152,192]{0,1:T(8,128)(2,1)S(1)}, bf16[1152,192]{0,1:T(8,128)(2,1)}, u32[]{:S(2)}, u32[]{:S(2)}) collective-permute-start(bf16[1152,192]{0,1:T(8,128)(2,1)S(1)} %convolution_convert_fusion.4), channel_id=1, source_target_pairs={{0,1},{1,0},{2,3},{3,2},{4,5},{5,4},{6,7},{7,6},{8,9},{9,8},{10,11... | collective-permute-start | bytes 1327112 | tf_op jit(solution)/shard_map/ppermute | solution.py:46
  146.2 6.3 %copy-start.2 = (bf16[1152,2560]{1,0:T(8,128)(2,1)S(1)}, bf16[1152,2560]{1,0:T(8,128)(2,1)}, u32[]{:S(2)}) copy-start(bf16[1152,2560]{1,0:T(8,128)(2,1)} %all-gather.3.cloned.1.call-done) | copy-start | bytes 17694724
  151.1 11.6 %collective-permute-start = (bf16[1152,192]{0,1:T(8,128)(2,1)S(1)}, bf16[1152,192]{0,1:T(8,128)(2,1)S(1)}, u32[]{:S(2)}, u32[]{:S(2)}) collective-permute-start(bf16[1152,192]{0,1:T(8,128)(2,1)S(1)} %convolution_convert_fusion.6), channel_id=1, source_target_pairs={{0,1},{1,0},{2,3},{3,2},{4,5},{5,4},{6,7},{7,6},{8,9},{9,8},{10,11... | collective-permute-start | bytes 1327112 | tf_op jit(solution)/shard_map/ppermute | solution.py:46
  154.5 17.6 %collective-permute-start.1 = (bf16[1152,192]{0,1:T(8,128)(2,1)S(1)}, bf16[1152,192]{0,1:T(8,128)(2,1)S(1)}, u32[]{:S(2)}, u32[]{:S(2)}) collective-permute-start(bf16[1152,192]{0,1:T(8,128)(2,1)S(1)} %convolution_convert_fusion.5), channel_id=1, source_target_pairs={{0,1},{1,0},{2,3},{3,2},{4,5},{5,4},{6,7},{7,6},{8,9},{9,8},{10,11... | collective-permute-start | bytes 1327112 | tf_op jit(solution)/shard_map/ppermute | solution.py:46
  174.0 4.6 %copy-start.3 = (bf16[1152,192]{0,1:T(8,128)(2,1)}, bf16[1152,192]{0,1:T(8,128)(2,1)S(1)}, u32[]{:S(2)}) copy-start(bf16[1152,192]{0,1:T(8,128)(2,1)S(1)} %get-tuple-element.8) | copy-start | bytes 1327108
  174.0 7.2 %copy-start.5 = (bf16[1152,192]{0,1:T(8,128)(2,1)}, bf16[1152,192]{0,1:T(8,128)(2,1)S(1)}, u32[]{:S(2)}) copy-start(bf16[1152,192]{0,1:T(8,128)(2,1)S(1)} %get-tuple-element.7) | copy-start | bytes 1327108
  178.3 1.2 copy-start.8
  178.3 89.4 %reduce-scatter.9.cloned.1.call-start = ((), (), s32[]{:S(2)}) async-start(), calls=%async_computation.12 | async-start | bytes 6635520 | tf_op jit(solution)/shard_map/reduce_scatter | solution.py:50
  179.5 1.8 copy-start.10
  224.0 46.2 %all-to-all-start.1 = ((bf16[16,9,2560]{2,1,0:T(8,128)(2,1)}), bf16[16,9,2560]{2,1,0:T(8,128)(2,1)}, u32[]{:S(2)}, u32[]{:S(2)}) async-start(bf16[16,9,2560]{2,1,0:T(8,128)(2,1)} %reshape.98), calls=%async_computation.2 | async-start | bytes 2621440 | tf_op jit(solution)/shard_map/all_to_all | solution.py:53
  270.2 41.8 %all-to-all-start.3 = ((bf16[16,9,2560]{2,1,0:T(8,128)(2,1)}), bf16[16,9,2560]{2,1,0:T(8,128)(2,1)S(1)}, u32[]{:S(2)}, u32[]{:S(2)}) async-start(bf16[16,9,2560]{2,1,0:T(8,128)(2,1)} %reshape.102), calls=%async_computation.6 | async-start | bytes 2621440 | tf_op jit(solution)/shard_map/all_to_all | solution.py:53
  279.5 45.1 %reduce-scatter.7.cloned.1.call-start = ((), (), s32[]{:S(2)}) async-start(), calls=%async_computation.10 | async-start | bytes 737280 | tf_op jit(solution)/shard_map/reduce_scatter | solution.py:63
  282.4 69.7 %reduce-scatter.11.cloned.1.call-start = ((), (), s32[]{:S(2)}) async-start(), calls=%async_computation.13 | async-start | bytes 737280 | tf_op jit(solution)/shard_map/reduce_scatter | solution.py:63
  312.3 6.8 %slice-start = ((s8[5898240]{0:T(1024)(128)(4,1)}), s8[1703936]{0:T(1024)(128)(4,1)S(1)}, s32[]{:S(2)}) async-start(s8[5898240]{0:T(1024)(128)(4,1)} %bitcast.64), calls=%async_computation.14 | async-start | bytes 3407872
  313.6 5.6 %slice-start.1 = ((s8[5898240]{0:T(1024)(128)(4,1)}), s8[4194304]{0:T(1024)(128)(4,1)S(1)}, s32[]{:S(2)}) async-start(s8[5898240]{0:T(1024)(128)(4,1)} %bitcast.64), calls=%async_computation.15 | async-start | bytes 8388608
  313.6 5.6 %copy-start.6 = (bf16[1152,192]{0,1:T(8,128)(2,1)S(1)}, bf16[1152,192]{0,1:T(8,128)(2,1)}, u32[]{:S(2)}) copy-start(bf16[1152,192]{0,1:T(8,128)(2,1)} %copy-done.5) | copy-start | bytes 1327108
  319.2 2.7 copy-start.4
  319.2 50.8 %copy-start.1 = (bf16[1,192,2560]{2,1,0:T(8,128)(2,1)S(1)}, bf16[1,192,2560]{2,1,0:T(8,128)(2,1)}, u32[]{:S(2)}) copy-start(bf16[1,192,2560]{2,1,0:T(8,128)(2,1)} %param.12) | copy-start | bytes 2949124
Sparse Core Ops, SparseCore 0:
  61.9 39.8 all-gather.4
  104.3 41.8 all-gather.2
  178.4 43.0 reduce-scatter.4
  224.1 43.5 reduce-scatter.8
  283.2 33.1 reduce-scatter.6
  319.3 32.7 reduce-scatter.10
where the time goes:
time: 378 us; the launch traced here: 377 us
  waiting for transfers between devices  165 us (44%)
  blocking collectives  111 us (29%)
  matrix products  38.2 us (10%)
  starting transfers between devices  25.7 us (7%)
  local copies, waits for them, and re-layouts  15.4 us (4%)
  between operations  14.4 us (4%)
  other arithmetic  6.83 us (2%)
    all_to_all x2, blocking collectives, dispatch(): lax.all_to_all(rows.reshape(dp_count, share_rows, half_width), 'dp', spli...  78 us
    reduce_scatter x2, waiting for transfers between devices, home(): lax.psum_scatter(partial_rows.astype(jnp.bfloat16), 'expert', scatter_dim...  70.4 us
    all_gather x2, waiting for transfers between devices, dispatch(): lax.all_gather(arrived.reshape(own_rows, half_width), 'expert', axis=0, t...  37.2 us
    dot_general x11, matrix products, mm(): return lax.dot_general(a, b, dims, preferred_element_type=jnp.float32)  35.3 us
    all_gather x2, blocking collectives, token_sum(): return lax.all_gather(part, 'expert', axis=0, tiled=True)  33.3 us
    all_to_all x2, waiting for transfers between devices, home(): lax.all_to_all(summed.reshape(dp_count, share_rows, half_width), 'dp', sp...  29.5 us
    all_to_all x2, starting transfers between devices, home(): lax.all_to_all(summed.reshape(dp_count, share_rows, half_width), 'dp', sp...  18.6 us
    ppermute x3, waiting for transfers between devices, width_sum(): other = lax.ppermute(mine, 'tensor', [(0, 1), (1, 0)])  17.4 us
  transfers between devices with their start and end apart: 11, of which 8 were waited for; matrix products, arithmetic and copies ran while one was open for 11% of the time, Pallas kernels for 0%

commit v1 on v0

--- a/solution.py
+++ b/solution.py
@@ -2,6 +2,11 @@
 import jax.numpy as jnp
 from jax import lax
 from jax.sharding import PartitionSpec as P
+
+
+def gather_over(x, name, along):
+    sent = jnp.stack([x] * lax.axis_size(name))
+    return jnp.concatenate(lax.all_to_all(sent, name, 0, 0), axis=along)
 
 
 def body(tokens, routes, route_weights, gate_weight, up_weight, down_weight, cotangent):
@@ -39,7 +44,7 @@
             concat_axis=0,
             tiled=True,
         )
-        return lax.all_gather(arrived.reshape(own_rows, half_width), "expert", axis=0, tiled=True)
+        return gather_over(arrived.reshape(own_rows, half_width), "expert", 0)
 
     def width_sum(partial_values):
         mine = partial_values.astype(jnp.bfloat16)

time: 378 us -> 468 us (1.24)
  waiting for transfers between devices: 165 us -> 284 us
  blocking collectives: 111 us -> 33.9 us
  starting transfers between devices: 25.7 us -> 59.4 us
  matrix products: 38.2 us -> 47.6 us
  local copies, waits for them, and re-layouts: 15.4 us -> 21.7 us
    all_to_all x0 -> x4, waiting for transfers between devices: none -> 176 us  [the longest x2 120 us: gather_over(): return jnp.concatenate(lax.all_to_all(sent, name, 0, 0), axis=along)]
    all_to_all x2 -> x0, blocking collectives: 78 us -> none  [dispatch(): lax.all_to_all(rows.reshape(dp_count, share_rows, half_width), 'dp', spli...]
    all_to_all x0 -> x4, starting transfers between devices: none -> 38.9 us  [the longest x2 19.6 us: dispatch(): lax.all_to_all(rows.reshape(dp_count, share_rows, half_width), 'dp', spli...]
    all_gather x2 -> x0, waiting for transfers between devices: 37.2 us -> none  [dispatch(): lax.all_gather(arrived.reshape(own_rows, half_width), 'expert', axis=0, t...]
    dot_general x11, matrix products: 35.3 us -> 44.8 us  [mm(): return lax.dot_general(a, b, dims, preferred_element_type=jnp.float32)]
    another operation x0 -> x4, local copies, waits for them, and re-layouts: none -> 8.05 us  [gather_over(): sent = jnp.stack([x] * lax.axis_size(name))]
    ppermute x3, waiting for transfers between devices: 17.4 us -> 10 us  [width_sum(): other = lax.ppermute(mine, 'tensor', [(0, 1), (1, 0)])]
    reduce_scatter x2, waiting for transfers between devices: 10.3 us -> 4.09 us  [token_sum(): lax.psum_scatter(partial_tokens.astype(jnp.bfloat16), 'expert', scatter_d...]
  transfers between devices with their start and end apart: 11 -> 13, of which waited for: 8 -> 9; matrix products, arithmetic and copies ran while one was open for 11% -> 11% of each run, Pallas kernels for 0% -> 0%
where the time goes in v1:
time: 468 us; the launch traced here: 467 us
  waiting for transfers between devices  284 us (61%)
  starting transfers between devices  59.4 us (13%)
  matrix products  47.6 us (10%)
  blocking collectives  33.9 us (7%)
  local copies, waits for them, and re-layouts  21.7 us (5%)
  between operations  13.9 us (3%)
  other arithmetic  6.41 us (1%)
    all_to_all x2, waiting for transfers between devices, gather_over(): return jnp.concatenate(lax.all_to_all(sent, name, 0, 0), axis=along)  120 us
    reduce_scatter x2, waiting for transfers between devices, home(): lax.psum_scatter(partial_rows.astype(jnp.bfloat16), 'expert', scatter_dim...  64.7 us
    all_to_all x2, waiting for transfers between devices, dispatch(): lax.all_to_all(rows.reshape(dp_count, share_rows, half_width), 'dp', spli...  55.8 us
    dot_general x11, matrix products, mm(): return lax.dot_general(a, b, dims, preferred_element_type=jnp.float32)  44.8 us
    all_gather x2, blocking collectives, token_sum(): return lax.all_gather(part, 'expert', axis=0, tiled=True)  33.9 us
    all_to_all x2, waiting for transfers between devices, home(): lax.all_to_all(summed.reshape(dp_count, share_rows, half_width), 'dp', sp...  29.5 us
    all_to_all x2, starting transfers between devices, dispatch(): lax.all_to_all(rows.reshape(dp_count, share_rows, half_width), 'dp', spli...  19.6 us
    all_to_all x2, starting transfers between devices, gather_over(): return jnp.concatenate(lax.all_to_all(sent, name, 0, 0), axis=along)  19.2 us
  transfers between devices with their start and end apart: 13, of which 9 were waited for; matrix products, arithmetic and copies ran while one was open for 11% of the time, Pallas kernels for 0%

profile of v1, /device:TPU:1, one launch (start us, length us, event | category | flops | bytes accessed | tf_op | source)
XLA Modules:
  0.0 467.2 jit_solution(15004446328463177612)
XLA Ops:
  7.2 0.0 copy-start
  7.2 0.8 fusion.12
  8.0 1.7 reduce-window.6
  9.7 0.3 slice_reduce_fusion
  10.0 0.8 fusion.11
  10.7 0.7 bitcast_add_fusion
  11.4 0.1 compare_reduce_fusion
  11.6 1.4 convolution_convert_fusion.1
  13.0 1.4 reshape.100
  14.4 11.7 %all-to-all-start = ((bf16[16,9,2560]{2,1,0:T(8,128)(2,1)}), bf16[16,9,2560]{2,1,0:T(8,128)(2,1)S(1)}, u32[]{:S(2)}, u32[]{:S(2)}) async-start(bf16[16,9,2560]{2,1,0:T(8,128)(2,1)} %reshape.100), calls=%async_computation | async-start | bytes 2621440 | tf_op jit(solution)/shard_map/all_to_all | solution.py:40
  26.1 0.2 select_reduce_fusion
  26.3 1.4 fusion.1
  27.8 1.4 reshape.104
  29.1 27.5 %all-to-all-done = bf16[16,9,2560]{2,1,0:T(8,128)(2,1)S(1)} async-done(((bf16[16,9,2560]{2,1,0:T(8,128)(2,1)}), bf16[16,9,2560]{2,1,0:T(8,128)(2,1)S(1)}, u32[]{:S(2)}, u32[]{:S(2)}) %all-to-all-start) | async-done | bytes 737312 | tf_op jit(solution)/shard_map/all_to_all | solution.py:40
  56.6 7.9 %all-to-all-start.3 = ((bf16[16,9,2560]{2,1,0:T(8,128)(2,1)}), bf16[16,9,2560]{2,1,0:T(8,128)(2,1)}, u32[]{:S(2)}, u32[]{:S(2)}) async-start(bf16[16,9,2560]{2,1,0:T(8,128)(2,1)} %reshape.104), calls=%async_computation.5 | async-start | bytes 2621440 | tf_op jit(solution)/shard_map/all_to_all | solution.py:40
  64.5 0.3 stack_reshape.4
  64.8 28.3 %all-to-all-done.3 = bf16[16,9,2560]{2,1,0:T(8,128)(2,1)} async-done(((bf16[16,9,2560]{2,1,0:T(8,128)(2,1)}), bf16[16,9,2560]{2,1,0:T(8,128)(2,1)}, u32[]{:S(2)}, u32[]{:S(2)}) %all-to-all-start.3) | async-done | bytes 737312 | tf_op jit(solution)/shard_map/all_to_all | solution.py:40
  93.1 3.1 stack.6
  96.2 13.6 %all-to-all-start.1 = ((bf16[8,144,2560]{2,1,0:T(8,128)(2,1)}), bf16[8,144,2560]{2,1,0:T(8,128)(2,1)}, u32[]{:S(2)}, u32[]{:S(2)}) async-start(bf16[8,144,2560]{2,1,0:T(8,128)(2,1)} %stack.6), calls=%async_computation.1 | async-start | bytes 11796480 | tf_op jit(solution)/shard_map/all_to_all | solution.py:9
  109.8 1.6 stack_reshape.5
  111.5 65.6 %all-to-all-done.1 = bf16[8,144,2560]{2,1,0:T(8,128)(2,1)} async-done(((bf16[8,144,2560]{2,1,0:T(8,128)(2,1)}), bf16[8,144,2560]{2,1,0:T(8,128)(2,1)}, u32[]{:S(2)}, u32[]{:S(2)}) %all-to-all-start.1) | async-done | bytes 5898272 | tf_op jit(solution)/shard_map/all_to_all | solution.py:9
  177.0 3.0 stack.7
  180.1 5.6 %all-to-all-start.4 = ((bf16[8,144,2560]{2,1,0:T(8,128)(2,1)}), bf16[8,144,2560]{2,1,0:T(8,128)(2,1)}, u32[]{:S(2)}, u32[]{:S(2)}) async-start(bf16[8,144,2560]{2,1,0:T(8,128)(2,1)} %stack.7), calls=%async_computation.6 | async-start | bytes 11796480 | tf_op jit(solution)/shard_map/all_to_all | solution.py:9
  185.7 5.6 %convolution_convert_fusion.6 = bf16[1152,192]{0,1:T(8,128)(2,1)} fusion(bf16[1152,2560]{1,0:T(8,128)(2,1)} %bitcast.5, bf16[1,192,2560]{2,1,0:T(8,128)(2,1)S(1)} %copy-done.2), kind=kOutput, calls=%fused_computation.13 | convolution fusion | flops 1132683264 | bytes 7323648 | tf_op jit(solution)/shard_map/dot_general | solution.py:80
  191.2 5.5 %convolution_convert_fusion.5 = bf16[1152,192]{0,1:T(8,128)(2,1)} fusion(bf16[1152,2560]{1,0:T(8,128)(2,1)} %bitcast.5, bf16[1,192,2560]{2,1,0:T(8,128)(2,1)S(1)} %copy-done.3), kind=kOutput, calls=%fused_computation.12 | convolution fusion | flops 1132683264 | bytes 7323648 | tf_op jit(solution)/shard_map/dot_general | solution.py:80
  196.7 1.5 collective-permute-start.1
  198.2 54.6 %all-to-all-done.4 = bf16[8,144,2560]{2,1,0:T(8,128)(2,1)} async-done(((bf16[8,144,2560]{2,1,0:T(8,128)(2,1)}), bf16[8,144,2560]{2,1,0:T(8,128)(2,1)}, u32[]{:S(2)}, u32[]{:S(2)}) %all-to-all-start.4) | async-done | bytes 5898272 | tf_op jit(solution)/shard_map/all_to_all | solution.py:9
  252.8 4.7 %convolution_convert_fusion.4 = bf16[1152,192]{0,1:T(8,128)(2,1)S(1)} fusion(bf16[1152,2560]{1,0:T(8,128)(2,1)} %bitcast.9, bf16[1,192,2560]{2,1,0:T(8,128)(2,1)S(1)} %copy-done), kind=kOutput, calls=%fused_computation.11 | convolution fusion | flops 1132683264 | bytes 7323648 | tf_op jit(solution)/shard_map/dot_general | solution.py:80
  257.6 0.1 collective-permute-start.2
  257.7 0.0 collective-permute-done
  257.7 0.0 copy-start.5
  257.7 0.8 copy-done.5
  258.5 10.0 %collective-permute-done.2 = bf16[1152,192]{0,1:T(8,128)(2,1)S(1)} collective-permute-done((bf16[1152,192]{0,1:T(8,128)(2,1)S(1)}, bf16[1152,192]{0,1:T(8,128)(2,1)S(1)}, u32[]{:S(2)}, u32[]{:S(2)}) %collective-permute-start.2) | collective-permute-done | bytes 442400 | tf_op jit(solution)/shard_map/ppermute | solution.py:51
  268.5 2.1 multiply_convert_fusion
  270.6 4.3 convolution_convert_fusion
  274.8 0.0 reduce-scatter.5.cloned.1.call-update
  274.9 0.2 reduce-scatter.9.cloned.1.call-start
  275.1 0.0 copy-start.4
  275.1 1.7 fusion.6
  276.9 4.3 fusion
  281.1 0.0 reduce-scatter.9.cloned.1.call-update
  281.1 30.0 %reduce-scatter.5.cloned.1.call-done = bf16[144,2560]{1,0:T(8,128)(2,1)} async-done(((bf16[1152,2560]{1,0:T(8,128)(2,1)}), bf16[144,2560]{1,0:T(8,128)(2,1)}) %reduce-scatter.5.cloned.1.call-update) | async-done | bytes 737296 | tf_op jit(solution)/shard_map/reduce_scatter | solution.py:55
  311.2 2.5 reshape.102
  313.6 9.3 %all-to-all-start.2 = ((bf16[16,9,2560]{2,1,0:T(8,128)(2,1)}), bf16[16,9,2560]{2,1,0:T(8,128)(2,1)}, u32[]{:S(2)}, u32[]{:S(2)}) async-start(bf16[16,9,2560]{2,1,0:T(8,128)(2,1)} %reshape.102), calls=%async_computation.3 | async-start | bytes 2621440 | tf_op jit(solution)/shard_map/all_to_all | solution.py:58
  323.0 34.7 %reduce-scatter.9.cloned.1.call-done = bf16[144,2560]{1,0:T(8,128)(2,1)} async-done(((bf16[1152,2560]{1,0:T(8,128)(2,1)}), bf16[144,2560]{1,0:T(8,128)(2,1)}) %reduce-scatter.9.cloned.1.call-update) | async-done | bytes 737296 | tf_op jit(solution)/shard_map/reduce_scatter | solution.py:55
  357.6 2.5 reshape.106
  360.1 9.3 %all-to-all-start.5 = ((bf16[16,9,2560]{2,1,0:T(8,128)(2,1)}), bf16[16,9,2560]{2,1,0:T(8,128)(2,1)}, u32[]{:S(2)}, u32[]{:S(2)}) async-start(bf16[16,9,2560]{2,1,0:T(8,128)(2,1)} %reshape.106), calls=%async_computation.8 | async-start | bytes 2621440 | tf_op jit(solution)/shard_map/all_to_all | solution.py:58
  369.4 0.0 reduce-scatter.7.cloned.1.call-start
  369.5 1.6 reshape.103
  371.1 1.2 convolution_convert_fusion.3
  372.3 0.0 reduce-scatter.7.cloned.1.call-update
  372.4 0.0 reduce-scatter.11.cloned.1.call-start
  372.4 29.5 %all-to-all-done.5 = bf16[16,9,2560]{2,1,0:T(8,128)(2,1)} async-done(((bf16[16,9,2560]{2,1,0:T(8,128)(2,1)}), bf16[16,9,2560]{2,1,0:T(8,128)(2,1)}, u32[]{:S(2)}, u32[]{:S(2)}) %all-to-all-start.5) | async-done | bytes 737312 | tf_op jit(solution)/shard_map/all_to_all | solution.py:58
  401.9 1.6 reshape.107
  403.5 1.2 convolution_convert_fusion.2
  404.8 0.0 reduce-scatter.11.cloned.1.call-update
  404.8 5.4 %convolution_bitcast_fusion = f32[1,192,2560]{2,1,0:T(8,128)} fusion(bf16[1152,192]{0,1:T(8,128)(2,1)S(1)} %get-tuple-element.9, bf16[1152,2560]{1,0:T(8,128)(2,1)} %bitcast.9), kind=kOutput, calls=%fused_computation.3 | convolution fusion | flops 1132462080 | bytes 8306688 | tf_op jit(solution)/shard_map/dot_general | solution.py:80
  410.2 5.5 %convolution_bitcast_fusion.1 = f32[1,192,2560]{2,1,0:T(8,128)} fusion(bf16[1152,192]{0,1:T(8,128)(2,1)S(1)} %get-tuple-element.7, bf16[1152,2560]{1,0:T(8,128)(2,1)} %bitcast.5), kind=kOutput, calls=%fused_computation.4 | convolution fusion | flops 1132462080 | bytes 8306688 | tf_op jit(solution)/shard_map/dot_general | solution.py:80
  415.7 5.4 %convolution_bitcast_fusion.2 = f32[1,192,2560]{2,1,0:T(8,128)} fusion(bf16[1152,192]{0,1:T(8,128)(2,1)S(1)} %get-tuple-element.8, bf16[1152,2560]{1,0:T(8,128)(2,1)} %bitcast.5), kind=kOutput, calls=%fused_computation.5 | convolution fusion | flops 1132462080 | bytes 8306688 | tf_op jit(solution)/shard_map/dot_general | solution.py:80
  421.1 17.3 %all_gather.6 = bf16[128,2560]{1,0:T(8,128)(2,1)S(1)} all-gather(bf16[16,2560]{1,0:T(8,128)(2,1)} %reduce-scatter.7.cloned.1.call-done), channel_id=1, replica_groups=mesh['dp'=16,'expert'=8,'tensor'=2] {'expert'}, dimensions={0}, use_global_device_ids=true | all-gather | bytes 737280 | tf_op jit(solution)/shard_map/all_gather | solution.py:71
  438.4 4.1 reduce-scatter.11.cloned.1.call-done
  442.5 16.5 %all_gather.7 = bf16[128,2560]{1,0:T(8,128)(2,1)S(1)} all-gather(bf16[16,2560]{1,0:T(8,128)(2,1)} %reduce-scatter.11.cloned.1.call-done), channel_id=1, replica_groups=mesh['dp'=16,'expert'=8,'tensor'=2] {'expert'}, dimensions={0}, use_global_device_ids=true | all-gather | bytes 737280 | tf_op jit(solution)/shard_map/all_gather | solution.py:71
  459.0 0.8 copy.18
  459.9 0.8 copy.19
  (17 shorter events, 0.1 us)
Async XLA Ops:
  7.2 245.7 %copy-start = (bf16[1,192,2560]{2,1,0:T(8,128)(2,1)S(1)}, bf16[1,192,2560]{2,1,0:T(8,128)(2,1)}, u32[]{:S(2)}) copy-start(bf16[1,192,2560]{2,1,0:T(8,128)(2,1)} %param.12) | copy-start | bytes 2949124
  7.2 18.9 %copy-start.6 = (f32[128,6]{0,1:T(8,128)S(1)}, f32[128,6]{0,1:T(8,128)}, u32[]{:S(2)}) copy-start(f32[128,6]{0,1:T(8,128)} %param.9) | copy-start | bytes 9220
  14.4 42.3 %all-to-all-start = ((bf16[16,9,2560]{2,1,0:T(8,128)(2,1)}), bf16[16,9,2560]{2,1,0:T(8,128)(2,1)S(1)}, u32[]{:S(2)}, u32[]{:S(2)}) async-start(bf16[16,9,2560]{2,1,0:T(8,128)(2,1)} %reshape.100), calls=%async_computation | async-start | bytes 2621440 | tf_op jit(solution)/shard_map/all_to_all | solution.py:40
  56.6 36.5 %all-to-all-start.3 = ((bf16[16,9,2560]{2,1,0:T(8,128)(2,1)}), bf16[16,9,2560]{2,1,0:T(8,128)(2,1)}, u32[]{:S(2)}, u32[]{:S(2)}) async-start(bf16[16,9,2560]{2,1,0:T(8,128)(2,1)} %reshape.104), calls=%async_computation.5 | async-start | bytes 2621440 | tf_op jit(solution)/shard_map/all_to_all | solution.py:40
  96.2 80.8 %all-to-all-start.1 = ((bf16[8,144,2560]{2,1,0:T(8,128)(2,1)}), bf16[8,144,2560]{2,1,0:T(8,128)(2,1)}, u32[]{:S(2)}, u32[]{:S(2)}) async-start(bf16[8,144,2560]{2,1,0:T(8,128)(2,1)} %stack.6), calls=%async_computation.1 | async-start | bytes 11796480 | tf_op jit(solution)/shard_map/all_to_all | solution.py:9
  180.0 5.6 %copy-start.2 = (bf16[1,192,2560]{2,1,0:T(8,128)(2,1)S(1)}, bf16[1,192,2560]{2,1,0:T(8,128)(2,1)}, u32[]{:S(2)}) copy-start(bf16[1,192,2560]{2,1,0:T(8,128)(2,1)} %param.10) | copy-start | bytes 2949124
  180.1 72.8 %all-to-all-start.4 = ((bf16[8,144,2560]{2,1,0:T(8,128)(2,1)}), bf16[8,144,2560]{2,1,0:T(8,128)(2,1)}, u32[]{:S(2)}, u32[]{:S(2)}) async-start(bf16[8,144,2560]{2,1,0:T(8,128)(2,1)} %stack.7), calls=%async_computation.6 | async-start | bytes 11796480 | tf_op jit(solution)/shard_map/all_to_all | solution.py:9
  185.6 5.6 %copy-start.3 = (bf16[1,192,2560]{2,1,0:T(8,128)(2,1)S(1)}, bf16[1,192,2560]{2,1,0:T(8,128)(2,1)}, u32[]{:S(2)}) copy-start(bf16[1,192,2560]{2,1,0:T(8,128)(2,1)} %param.11) | copy-start | bytes 2949124
  185.7 125.5 %reduce-scatter.5.cloned.1.call-start = ((), (), s32[]{:S(2)}) async-start(), calls=%async_computation.10 | async-start | bytes 6635520 | tf_op jit(solution)/shard_map/reduce_scatter | solution.py:55
  191.2 66.4 %collective-permute-start = (bf16[1152,192]{0,1:T(8,128)(2,1)}, bf16[1152,192]{0,1:T(8,128)(2,1)}, u32[]{:S(2)}, u32[]{:S(2)}) collective-permute-start(bf16[1152,192]{0,1:T(8,128)(2,1)} %convolution_convert_fusion.6), channel_id=1, source_target_pairs={{0,1},{1,0},{2,3},{3,2},{4,5},{5,4},{6,7},{7,6},{8,9},{9,8},{10,11... | collective-permute-start | bytes 1327112 | tf_op jit(solution)/shard_map/ppermute | solution.py:51
  196.7 60.9 %collective-permute-start.1 = (bf16[1152,192]{0,1:T(8,128)(2,1)}, bf16[1152,192]{0,1:T(8,128)(2,1)S(1)}, u32[]{:S(2)}, u32[]{:S(2)}) collective-permute-start(bf16[1152,192]{0,1:T(8,128)(2,1)} %convolution_convert_fusion.5), channel_id=1, source_target_pairs={{0,1},{1,0},{2,3},{3,2},{4,5},{5,4},{6,7},{7,6},{8,9},{9,8},{10,11... | collective-permute-start | bytes 1327112 | tf_op jit(solution)/shard_map/ppermute | solution.py:51
  257.6 10.9 %collective-permute-start.2 = (bf16[1152,192]{0,1:T(8,128)(2,1)S(1)}, bf16[1152,192]{0,1:T(8,128)(2,1)S(1)}, u32[]{:S(2)}, u32[]{:S(2)}) collective-permute-start(bf16[1152,192]{0,1:T(8,128)(2,1)S(1)} %convolution_convert_fusion.4), channel_id=1, source_target_pairs={{0,1},{1,0},{2,3},{3,2},{4,5},{5,4},{6,7},{7,6},{8,9},{9,8},{10,11... | collective-permute-start | bytes 1327112 | tf_op jit(solution)/shard_map/ppermute | solution.py:51
  257.7 0.8 copy-start.5
  274.9 82.7 %reduce-scatter.9.cloned.1.call-start = ((), (), s32[]{:S(2)}) async-start(), calls=%async_computation.12 | async-start | bytes 6635520 | tf_op jit(solution)/shard_map/reduce_scatter | solution.py:55
  275.1 1.8 copy-start.4
  313.6 46.4 %all-to-all-start.2 = ((bf16[16,9,2560]{2,1,0:T(8,128)(2,1)}), bf16[16,9,2560]{2,1,0:T(8,128)(2,1)}, u32[]{:S(2)}, u32[]{:S(2)}) async-start(bf16[16,9,2560]{2,1,0:T(8,128)(2,1)} %reshape.102), calls=%async_computation.3 | async-start | bytes 2621440 | tf_op jit(solution)/shard_map/all_to_all | solution.py:58
  360.1 41.8 %all-to-all-start.5 = ((bf16[16,9,2560]{2,1,0:T(8,128)(2,1)}), bf16[16,9,2560]{2,1,0:T(8,128)(2,1)}, u32[]{:S(2)}, u32[]{:S(2)}) async-start(bf16[16,9,2560]{2,1,0:T(8,128)(2,1)} %reshape.106), calls=%async_computation.8 | async-start | bytes 2621440 | tf_op jit(solution)/shard_map/all_to_all | solution.py:58
  369.4 51.6 %reduce-scatter.7.cloned.1.call-start = ((), (), s32[]{:S(2)}) async-start(), calls=%async_computation.11 | async-start | bytes 737280 | tf_op jit(solution)/shard_map/reduce_scatter | solution.py:68
  372.4 70.1 %reduce-scatter.11.cloned.1.call-start = ((), (), s32[]{:S(2)}) async-start(), calls=%async_computation.13 | async-start | bytes 737280 | tf_op jit(solution)/shard_map/reduce_scatter | solution.py:68
  410.2 50.5 %copy-start.1 = (bf16[1,192,2560]{2,1,0:T(8,128)(2,1)S(1)}, bf16[1,192,2560]{2,1,0:T(8,128)(2,1)}, u32[]{:S(2)}) copy-start(bf16[1,192,2560]{2,1,0:T(8,128)(2,1)} %param.12) | copy-start | bytes 2949124
Sparse Core Ops, SparseCore 0:
  275.0 36.1 reduce-scatter.4
  313.9 43.6 reduce-scatter.8
  373.4 33.4 reduce-scatter.6
  409.9 32.5 reduce-scatter.10
